TPU v7x, 256 devices: a whole 4x4x8 slice. The times are simulated.
256 devices in a mesh: pipe: 32 (over y_hi, z, core), ctx: 8 (over x, y_lo).
Axes of the slice: x: 4, y: 4 (y_hi: 2, y_lo: 2; y = y_hi * 2 + y_lo), z: 8, core: 2. Of those that a mesh axis runs over, the one named last changes fastest.
Arguments:
- query: bfloat16 [32, 1024, 8192], P('pipe', 'ctx'), may hold values from -6 to 6
- inner: bfloat16 [32, 1024, 8192], P('pipe', 'ctx'), may hold values from -6 to 6
- out_grad: bfloat16 [32, 1024, 8192], P('pipe', 'ctx'), may hold values from -6 to 6
- filters: float32 [32, 7, 8192], P('pipe'), as said below
- trace_lengths: int32 [32, 2], P('pipe'), may hold values from 1 to 960, 1024 in all within a row
Outputs:
- passed_grad: bfloat16 [2, 32, 1024, 8192], P(None, 'pipe', 'ctx')
- filter_grad: float32 [32, 7, 8192], P('pipe', None, 'ctx')
Inputs may be any that keep to these rules, and one draw needn't show every extreme that they name: filters of section s and section 31 - s are equal (the same layer).
All inputs are finite; a program needn't handle non-finite values.
Results may differ from a plain program's by a relative error of at most 0.0041.
Values may be sent and summed in bfloat16 or wider, within the bound.
No kernel may reach another device: no remote copies, remote signals or barrier semaphores. Data moves between devices by JAX's collectives and lax.ppermute only.
A program may use at most 128 MiB of HBM per device.

v0:
```python
import functools

import jax
import jax.numpy as jnp
from jax import lax
from jax.experimental import pallas as pl
from jax.experimental.pallas import tpu as pltpu
from jax.sharding import PartitionSpec as P


SUB = 8
LANES = 128
EDGE = 16
HALO = 8
RANGES = ((2, 1024), (3, 1024), (3, 1024))


def f32(x):
    return x.astype(jnp.float32)


def rounded_product(a, b):
    return f32((f32(a) * f32(b)).astype(jnp.bfloat16))


def tap_rows(f_ref, lanes, taps):
    return [jnp.broadcast_to(f_ref[j, :, lanes], (SUB, LANES)) for j in range(taps)]


def back_parts(ref, row, taps, since):
    out = []
    for j in range(taps):
        part = ref[pl.ds(row - j, SUB), :]
        if since is not None and j > 0:
            part = jnp.where((since < 0) | (since >= j), part, 0.0)
        out.append(part)
    return out


def ahead_parts(ref, row, taps, since):
    out = []
    for j in range(taps):
        part = ref[pl.ds(row + j, SUB), :]
        if since is not None and j > 0:
            part = jnp.where((since >= 0) | (since < -j), part, 0.0)
        out.append(part)
    return out


def weighted(parts, f_rows):
    total = f_rows[0] * parts[0]
    for part, row in zip(parts[1:], f_rows[1:], strict=True):
        total = total + row * part
    return total


def store_pair(ref, which, row, lanes, low, high):
    ref[which, pl.ds(row, 2 * SUB), lanes] = jnp.concatenate([low, high], axis=0).astype(jnp.bfloat16)


def boundary(lengths_ref, rows, ctx):
    return lengths_ref[0, 0] - ctx * rows


def by_boundary(cut, rows, taps, body, count):
    near = (cut > -taps) & (cut < rows + taps)

    @pl.when(near)
    def _():
        lax.fori_loop(0, count, functools.partial(body, True), 0)

    @pl.when(jnp.logical_not(near))
    def _():
        lax.fori_loop(0, count, functools.partial(body, False), 0)


def main_kernel(taps, lengths_ref, f_ref, q_ref, u_ref, g_ref, *rest):
    y_ref, dh_ref, _, u_rows, gz_rows = rest[-5:]
    rows, width = q_ref.shape
    n_tiles, n_edge = rows // SUB, EDGE // SUB
    cut = boundary(lengths_ref, rows, lax.axis_index("ctx"))

    def column(masked, i, carry):
        lanes = pl.ds(pl.multiple_of(i * LANES, LANES), LANES)
        row_id = lax.broadcasted_iota(jnp.int32, (SUB, LANES), 0)
        f_rows = tap_rows(f_ref, lanes, taps)
        for k in range(0, n_tiles, 2):
            two = pl.ds(k * SUB, 2 * SUB)
            u_rows[two, :] = f32(u_ref[two, lanes])
            gz_rows[two, :] = rounded_product(g_ref[two, lanes], q_ref[two, lanes])
        acc = [jnp.zeros((SUB, LANES), jnp.float32) for _ in range(taps)]
        for k in range(0, n_tiles, 2):
            g_two = f32(g_ref[pl.ds(k * SUB, 2 * SUB), lanes])
            grads_q, grads_u = [], []
            for half in range(2):
                row = (k + half) * SUB
                since = row_id + (row - cut) if masked else None
                if k >= n_edge:
                    parts = back_parts(u_rows, row, taps, since)
                    gz_here = gz_rows[pl.ds(row, SUB), :]
                    for j in range(taps):
                        acc[j] = acc[j] + gz_here * parts[j]
                    grads_q.append(g_two[half * SUB : (half + 1) * SUB] * weighted(parts, f_rows))
                if k < n_tiles - n_edge:
                    grads_u.append(weighted(ahead_parts(gz_rows, row, taps, since), f_rows))
            if grads_q:
                store_pair(y_ref, 0, (k - n_edge) * SUB, lanes, *grads_q)
            if grads_u:
                store_pair(y_ref, 1, k * SUB, lanes, *grads_u)
        for j in range(taps):
            dh_ref[0, pl.ds(j, 1), lanes] = jnp.sum(acc[j], axis=0, keepdims=True)
        return carry

    by_boundary(cut, rows, taps, column, width // LANES)


def edge_kernel(taps, rows, lengths_ref, f_ref, q_hbm, u_hbm, g_hbm, left, right, dh_in, y_hbm, dh_out, *scratch):
    q_lo, u_lo, g_lo, q_hi, g_hi, dh_sums, y_ref, u_rows, gz_rows, sems = scratch
    n_edge = EDGE // SUB
    per_shard = dh_in.shape[2] // LANES
    cut = boundary(lengths_ref, rows, lax.axis_index("ctx"))
    low, high = pl.ds(0, EDGE), pl.ds(rows - EDGE, EDGE)
    pairs = [
        (q_hbm.at[low], q_lo), (u_hbm.at[low], u_lo), (g_hbm.at[low], g_lo), (q_hbm.at[high], q_hi), (g_hbm.at[high], g_hi),
        (dh_in, dh_sums),
    ]
    copies = [pltpu.make_async_copy(src, dst, sems.at[n]) for n, (src, dst) in enumerate(pairs)]
    for copy in copies:
        copy.start()
    for copy in copies:
        copy.wait()

    def column(masked, i, carry):
        lanes = pl.ds(pl.multiple_of(i * LANES, LANES), LANES)
        dest = i // per_shard
        place = pl.ds(pl.multiple_of((i % per_shard) * LANES, LANES), LANES)
        row_id = lax.broadcasted_iota(jnp.int32, (SUB, LANES), 0)
        f_rows = tap_rows(f_ref, lanes, taps)
        u_rows[pl.ds(0, HALO), :] = f32(left[:, lanes])
        u_rows[pl.ds(HALO, EDGE), :] = f32(u_lo[:, lanes])
        gz_rows[pl.ds(0, EDGE), :] = rounded_product(g_hi[:, lanes], q_hi[:, lanes])
        gz_rows[pl.ds(EDGE, HALO), :] = f32(right[:, lanes])
        gz_lo = rounded_product(g_lo[:, lanes], q_lo[:, lanes])
        g_here = f32(g_lo[:, lanes])
        acc = [None] * taps
        grads_q, grads_u = [], []
        for k in range(n_edge):
            here = slice(k * SUB, (k + 1) * SUB)
            since = row_id + (k * SUB - cut) if masked else None
            parts = back_parts(u_rows, HALO + k * SUB, taps, since)
            for j in range(taps):
                term = gz_lo[here] * parts[j]
                acc[j] = term if k == 0 else acc[j] + term
            grads_q.append(g_here[here] * weighted(parts, f_rows))
            since = row_id + (rows - EDGE + k * SUB - cut) if masked else None
            grads_u.append(weighted(ahead_parts(gz_rows, k * SUB, taps, since), f_rows))
        store_pair(y_ref, 0, 0, lanes, *grads_q)
        store_pair(y_ref, 1, 0, lanes, *grads_u)
        for j in range(taps):
            dh_sums[dest, pl.ds(j, 1), place] = dh_sums[dest, pl.ds(j, 1), place] + jnp.sum(acc[j], axis=0, keepdims=True)
        return carry

    by_boundary(cut, rows, taps, column, q_lo.shape[1] // LANES)
    copies = [pltpu.make_async_copy(y_ref, y_hbm, sems.at[0]), pltpu.make_async_copy(dh_sums, dh_out, sems.at[1])]
    for copy in copies:
        copy.start()
    for copy in copies:
        copy.wait()


ANYWHERE = pl.BlockSpec(memory_space=pl.ANY)
LONG = pl.CostEstimate(flops=1 << 34, bytes_accessed=1 << 20, transcendentals=0)
BRIEF = pl.CostEstimate(flops=1, bytes_accessed=1, transcendentals=0)
ON_CHIP = pl.BlockSpec(memory_space=pltpu.VMEM)
SCALARS = pl.BlockSpec(memory_space=pltpu.SMEM)


def main_part(lengths, f3, query, inner, out_grad, dh, shards, first, count, block):
    rows, width = query.shape
    taps = f3.shape[0]
    base = first // block
    per = width // shards // block
    wide = pl.BlockSpec((rows, block), lambda c: (0, base + c))
    return pl.pallas_call(
        functools.partial(main_kernel, taps),
        out_shape=(
            jax.ShapeDtypeStruct((2, rows - EDGE, count), jnp.bfloat16),
            jax.ShapeDtypeStruct((shards, taps, width // shards), jnp.float32),
            jax.ShapeDtypeStruct((2, 1, rows, width) if dh is None else (1, 1, SUB, LANES), jnp.bfloat16),
        ),
        grid=(count // block,),
        in_specs=[SCALARS, pl.BlockSpec((taps, 1, block), lambda c: (0, 0, base + c)), wide, wide, wide]
        + ([] if dh is None else [ANYWHERE]),
        out_specs=(
            pl.BlockSpec((2, rows - EDGE, block), lambda c: (0, 0, c)),
            pl.BlockSpec((1, taps, block), lambda c: ((base + c) // per, 0, (base + c) % per)),
            ANYWHERE,
        ),
        scratch_shapes=[pltpu.VMEM((rows, LANES), jnp.float32)] * 2,
        input_output_aliases={} if dh is None else {5: 1},
        cost_estimate=BRIEF,
        name=f"grads_{first}",
    )(lengths, f3, query, inner, out_grad, *([] if dh is None else [dh]))


def edge_part(lengths, f3, query, inner, out_grad, left, right, dh):
    rows, width = query.shape
    taps = f3.shape[0]
    edge = pltpu.VMEM((EDGE, width), jnp.bfloat16)
    return pl.pallas_call(
        functools.partial(edge_kernel, taps, rows),
        out_shape=(jax.ShapeDtypeStruct((2, EDGE, width), jnp.bfloat16), jax.ShapeDtypeStruct(dh.shape, dh.dtype)),
        in_specs=[SCALARS, ON_CHIP] + [ANYWHERE] * 3 + [ON_CHIP] * 2 + [ANYWHERE],
        out_specs=(ANYWHERE, ANYWHERE),
        scratch_shapes=[
            edge, edge, edge, edge, edge,
            pltpu.VMEM(dh.shape, dh.dtype),
            pltpu.VMEM((2, EDGE, width), jnp.bfloat16),
            pltpu.VMEM((HALO + EDGE, LANES), jnp.float32),
            pltpu.VMEM((HALO + EDGE, LANES), jnp.float32),
            pltpu.SemaphoreType.DMA((6,)),
        ],
        cost_estimate=BRIEF,
        name="edge_grads",
    )(lengths, f3, query, inner, out_grad, left, right, dh)


def put(out, y, spots):
    for k, (row, lane) in enumerate(spots):
        out = lax.dynamic_update_slice(out, y[k][None, None], (k, 0, row, lane))
    return out


def sent(x, axis, to):
    n = lax.axis_size(axis)
    return lax.ppermute(x, axis, [(i, to(i)) for i in range(n) if 0 <= to(i) < n])


def local(query, inner, out_grad, filters, trace_lengths):
    query, inner, out_grad = query[0], inner[0], out_grad[0]
    rows, width = query.shape
    f3 = jnp.transpose(filters, (1, 0, 2))
    shards = lax.axis_size("ctx")
    eighth = width // sum(part for part, _ in RANGES)

    first, dh, parts = 0, None, []
    for part, block in RANGES:
        count = part * eighth
        y, dh, blank = main_part(trace_lengths, f3, query, inner, out_grad, dh, shards, first, count, block)
        out = blank if first == 0 else out
        parts.append((first, y))
        first += count
    pipe, half = lax.axis_index("pipe"), lax.axis_size("pipe") // 2
    arrived = [(first, sent(y, "pipe", lambda i: i - 1)) for first, y in parts]
    y_two = parts[1][1]
    near = sent(y_two, "pipe", lambda i: 0 if i == half else i - 1 if i > 1 else -1)
    relay = jnp.where(pipe == 0, near, y_two)

    q_head, g_head, u_tail, _ = lax.optimization_barrier((query, out_grad, inner, parts[1][1]))
    left = sent(u_tail[rows - HALO :], "ctx", lambda i: i + 1)
    right = sent((f32(g_head[:HALO]) * f32(q_head[:HALO])).astype(jnp.bfloat16), "ctx", lambda i: i - 1)
    f0, y0 = arrived[0]
    out = put(out, y0, ((EDGE, f0), (0, f0)))
    y_edge, dh = edge_part(trace_lengths, f3, query, inner, out_grad, left, right, dh)
    edge = sent(y_edge, "pipe", lambda i: i - 1)

    dh, relay = lax.optimization_barrier((dh, relay))
    far = sent(relay, "pipe", lambda i: half - 1 if i == 0 else 0 if i == 1 else -1)
    shares = lax.all_to_all(dh, "ctx", split_axis=0, concat_axis=0, tiled=True)
    shares, out = lax.optimization_barrier((shares, out))
    arrived = [arrived[2], (arrived[1][0], jnp.where((pipe == 0) | (pipe == half - 1), far, near))]
    mine = jnp.sum(shares, axis=0)[None]
    last = lax.axis_size("pipe") - 1
    theirs = sent(mine, "pipe", lambda i: last - i)

    for first, y in arrived:
        out = put(out, y, ((EDGE, first), (0, first)))
    out = put(out, edge, ((0, 0), (rows - EDGE, 0)))
    mine, out = lax.optimization_barrier((mine, out))
    return out, mine + theirs


def solution(mesh):
    in_specs = (
        P("pipe", "ctx", None),
        P("pipe", "ctx", None),
        P("pipe", "ctx", None),
        P("pipe", None, None),
        P("pipe", None),
    )
    out_specs = (P(None, "pipe", "ctx", None), P("pipe", None, "ctx"))
    return jax.shard_map(local, mesh=mesh, in_specs=in_specs, out_specs=out_specs, check_vma=False)
```

profile of v0, /device:TPU:2, one launch (start us, length us, event | category | flops | bytes accessed | tf_op | source)
XLA Modules:
  0.0 80.9 jit_solution(5458491852937680599)
XLA Ops:
  0.6 4.0 %grads_0.1 = (bf16[2,112,2048]{2,1,0:T(8,128)(2,1)}, f32[8,7,1024]{2,1,0:T(8,128)}, bf16[2,1,128,8192]{3,2,1,0:T(8,128)(2,1)}) custom-call(s32[1,2]{1,0:T(1,128)} %lengths_ref.7, f32[7,1,8192]{2,1,0:T(1,128)} %bitcast.51, bf16[128,8192]{1,0:T(8,128)(2,1)} %bitcast.36, bf16[128,8192]{1,0:T(8,128)(2,1)} %bitcast.41, bf16[128,8192]{1,0:T(8,128)(2,1)} %bitcast.46), custom_call_target="tpu_custom_call" | custom-call | flops 1 | bytes 1 | tf_op jit(solution)/shard_map/grads_0/pallas_call | solution.py:184
  4.6 1.3 %collective-permute-start.3 = (bf16[2,112,2048]{2,1,0:T(8,128)(2,1)}, bf16[2,112,2048]{2,1,0:T(8,128)(2,1)}, u32[]{:S(2)}, u32[]{:S(2)}) collective-permute-start(bf16[2,112,2048]{2,1,0:T(8,128)(2,1)} %get-tuple-element.30), channel_id=1, source_target_pairs={{8,0},{16,8},{24,16},{32,24},{40,32},{48,40},{56,48},{64,56},{72,6... | collective-permute-start | bytes 2752520 | tf_op jit(solution)/shard_map/ppermute | solution.py:236
  5.9 5.3 %grads_2048.1 = (bf16[2,112,3072]{2,1,0:T(8,128)(2,1)}, f32[8,7,1024]{2,1,0:T(8,128)}, bf16[1,1,8,128]{3,2,1,0:T(8,128)(2,1)}) custom-call(s32[1,2]{1,0:T(1,128)} %lengths_ref.7, f32[7,1,8192]{2,1,0:T(1,128)} %bitcast.52, bf16[128,8192]{1,0:T(8,128)(2,1)} %bitcast.37, bf16[128,8192]{1,0:T(8,128)(2,1)} %bitcast.42, ...), custom_call_target="tpu_custom_call", output_to_operand_aliasing={{1}: (5, {})} | custom-call | flops 1 | bytes 1 | tf_op jit(solution)/shard_map/grads_2048/pallas_call | solution.py:184
  11.2 1.3 %collective-permute-start.2 = (bf16[2,112,3072]{2,1,0:T(8,128)(2,1)}, bf16[2,112,3072]{2,1,0:T(8,128)(2,1)S(1)}, u32[]{:S(2)}, u32[]{:S(2)}) collective-permute-start(bf16[2,112,3072]{2,1,0:T(8,128)(2,1)} %get-tuple-element.21), channel_id=1, source_target_pairs={{16,8},{24,16},{32,24},{40,32},{48,40},{56,48},{64,56},{72,64},{80... | collective-permute-start | bytes 4128776 | tf_op jit(solution)/shard_map/ppermute | solution.py:236
  12.5 1.0 %multiply_convert_fusion = bf16[8,8192]{1,0:T(8,128)(2,1)S(1)} fusion(bf16[128,8192]{1,0:T(8,128)(2,1)} %bitcast.38, bf16[128,8192]{1,0:T(8,128)(2,1)} %bitcast.48), kind=kLoop, calls=%fused_computation.18 | loop fusion | flops 262144 | bytes 393216 | tf_op jit(solution)/shard_map/convert_element_type | solution.py:261
  13.5 5.1 %collective-permute-start.1 = (bf16[8,8192]{1,0:T(8,128)(2,1)S(1)}, bf16[8,8192]{1,0:T(8,128)(2,1)S(1)}, u32[]{:S(2)}, u32[]{:S(2)}) collective-permute-start(bf16[8,8192]{1,0:T(8,128)(2,1)S(1)} %multiply_convert_fusion), channel_id=1, source_target_pairs={{1,0},{2,1},{3,2},{4,3},{5,4},{6,5},{7,6},{9,8},{10,9},{11,10},{12... | collective-permute-start | bytes 393224 | tf_op jit(solution)/shard_map/ppermute | solution.py:236
  18.6 0.9 %slice.33 = bf16[8,8192]{1,0:T(8,128)(2,1)S(1)} slice(bf16[128,8192]{1,0:T(8,128)(2,1)} %bitcast.43), slice={[120:128], [0:8192]} | slice | bytes 262144 | tf_op jit(solution)/shard_map/slice | solution.py:260
  19.5 1.9 %collective-permute-start = (bf16[8,8192]{1,0:T(8,128)(2,1)S(1)}, bf16[8,8192]{1,0:T(8,128)(2,1)S(1)}, u32[]{:S(2)}, u32[]{:S(2)}) collective-permute-start(bf16[8,8192]{1,0:T(8,128)(2,1)S(1)} %slice.33), channel_id=1, source_target_pairs={{0,1},{1,2},{2,3},{3,4},{4,5},{5,6},{6,7},{8,9},{9,10},{10,11},{11... | collective-permute-start | bytes 393224 | tf_op jit(solution)/shard_map/ppermute | solution.py:236
  21.5 5.3 %grads_5120.1 = (bf16[2,112,3072]{2,1,0:T(8,128)(2,1)}, f32[8,7,1024]{2,1,0:T(8,128)}, bf16[1,1,8,128]{3,2,1,0:T(8,128)(2,1)}) custom-call(s32[1,2]{1,0:T(1,128)} %lengths_ref.7, f32[7,1,8192]{2,1,0:T(1,128)} %bitcast.53, bf16[128,8192]{1,0:T(8,128)(2,1)} %bitcast.39, bf16[128,8192]{1,0:T(8,128)(2,1)} %bitcast.44, ...), custom_call_target="tpu_custom_call", output_to_operand_aliasing={{1}: (5, {})} | custom-call | flops 1 | bytes 1 | tf_op jit(solution)/shard_map/grads_5120/pallas_call | solution.py:184
  26.8 1.3 %collective-permute-start.4 = (bf16[2,112,3072]{2,1,0:T(8,128)(2,1)}, bf16[2,112,3072]{2,1,0:T(8,128)(2,1)S(1)}, u32[]{:S(2)}, u32[]{:S(2)}) collective-permute-start(bf16[2,112,3072]{2,1,0:T(8,128)(2,1)} %get-tuple-element.33), channel_id=1, source_target_pairs={{8,0},{16,8},{24,16},{32,24},{40,32},{48,40},{56,48},{64,56},{72,6... | collective-permute-start | bytes 4128776 | tf_op jit(solution)/shard_map/ppermute | solution.py:236
  28.8 5.7 %edge_grads.1 = (bf16[2,16,8192]{2,1,0:T(8,128)(2,1)}, f32[8,7,1024]{2,1,0:T(8,128)}) custom-call(s32[1,2]{1,0:T(1,128)} %lengths_ref.7, f32[7,1,8192]{2,1,0:T(1,128)} %bitcast.54, bf16[128,8192]{1,0:T(8,128)(2,1)} %bitcast.40, bf16[128,8192]{1,0:T(8,128)(2,1)} %bitcast.45, bf16[128,8192]{1,0:T(8,128)(2,1)} %bitcast.50, bf16[8,8192]{1,0:T(8,128)(2,1)} %copy-done.1, ...), custom_call_target="tpu_custom_call" | custom-call | flops 1 | bytes 1 | tf_op jit(solution)/shard_map/edge_grads/pallas_call | solution.py:210
  34.5 1.3 %collective-permute-start.6 = (bf16[2,16,8192]{2,1,0:T(8,128)(2,1)}, bf16[2,16,8192]{2,1,0:T(8,128)(2,1)S(1)}, u32[]{:S(2)}, u32[]{:S(2)}) collective-permute-start(bf16[2,16,8192]{2,1,0:T(8,128)(2,1)} %get-tuple-element.35), channel_id=1, source_target_pairs={{8,0},{16,8},{24,16},{32,24},{40,32},{48,40},{56,48},{64,56},{72,6... | collective-permute-start | bytes 1572872 | tf_op jit(solution)/shard_map/ppermute | solution.py:236
  35.8 1.8 %fusion.5 = bf16[2,1,128,8192]{3,2,1,0:T(8,128)(2,1)} fusion(bf16[2,1,128,8192]{3,2,1,0:T(8,128)(2,1)} %get-tuple-element.29, bf16[2,112,2048]{2,1,0:T(8,128)(2,1)} %collective-permute-done.3), kind=kLoop, calls=%fused_computation.13 | loop fusion | bytes 917504 | tf_op jit(solution)/shard_map/dynamic_update_slice | solution.py:230
  37.6 5.1 %collective-permute-done.2 = bf16[2,112,3072]{2,1,0:T(8,128)(2,1)S(1)} collective-permute-done((bf16[2,112,3072]{2,1,0:T(8,128)(2,1)}, bf16[2,112,3072]{2,1,0:T(8,128)(2,1)S(1)}, u32[]{:S(2)}, u32[]{:S(2)}) %collective-permute-start.2) | collective-permute-done | bytes 1376288 | tf_op jit(solution)/shard_map/ppermute | solution.py:236
  42.7 1.2 %broadcast_select_fusion.1 = bf16[2,112,3072]{2,1,0:T(8,128)(2,1)} fusion(bf16[2,112,3072]{2,1,0:T(8,128)(2,1)S(1)} %collective-permute-done.2, bf16[2,112,3072]{2,1,0:T(8,128)(2,1)} %get-tuple-element.21, pred[]{:T(512)S(6)} %eq.7), kind=kLoop, calls=%fused_computation.1 | loop fusion | flops 688128 | bytes 4128769 | tf_op jit(solution)/shard_map/jit(_where)/select_n | solution.py:257
  44.0 6.3 %all-to-all-start = ((f32[8,7,1024]{2,1,0:T(8,128)}), f32[8,7,1024]{2,1,0:T(8,128)S(1)}, u32[]{:S(2)}, u32[]{:S(2)}) async-start(f32[8,7,1024]{2,1,0:T(8,128)} %get-tuple-element.28), calls=%async_computation | async-start | bytes 524288 | tf_op jit(solution)/shard_map/all_to_all | solution.py:269
  50.3 1.8 %fusion.4 = bf16[2,1,128,8192]{3,2,1,0:T(8,128)(2,1)} fusion(bf16[2,1,128,8192]{3,2,1,0:T(8,128)(2,1)} %fusion.5, bf16[2,112,2048]{2,1,0:T(8,128)(2,1)} %collective-permute-done.3), kind=kLoop, calls=%fused_computation.11 | loop fusion | bytes 917504 | tf_op jit(solution)/shard_map/dynamic_update_slice | solution.py:230
  52.1 6.4 %collective-permute-start.5 = (bf16[2,112,3072]{2,1,0:T(8,128)(2,1)}, bf16[2,112,3072]{2,1,0:T(8,128)(2,1)}, u32[]{:S(2)}, u32[]{:S(2)}) collective-permute-start(bf16[2,112,3072]{2,1,0:T(8,128)(2,1)} %broadcast_select_fusion.1), channel_id=1, source_target_pairs={{0,120},{8,0},{1,121},{9,1},{2,122},{10,2},{3,123},{11,3},{4,124},... | collective-permute-start | bytes 4128776 | tf_op jit(solution)/shard_map/ppermute | solution.py:236
  60.0 8.9 %collective-permute-start.7 = (f32[1,7,1024]{2,0,1:T(1,128)S(1)}, f32[1,7,1024]{2,0,1:T(1,128)S(1)}, u32[]{:S(2)}, u32[]{:S(2)}) collective-permute-start(f32[1,7,1024]{2,0,1:T(1,128)S(1)} %broadcast_in_dim.3), channel_id=1, source_target_pairs={{0,248},{8,240},{16,232},{24,224},{32,216},{40,208},{48,200},{56,1... | collective-permute-start | bytes 86024 | tf_op jit(solution)/shard_map/ppermute | solution.py:236
  68.9 0.9 %fusion.3 = bf16[2,1,128,8192]{3,2,1,0:T(8,128)(2,1)} fusion(bf16[2,1,128,8192]{3,2,1,0:T(8,128)(2,1)} %fusion.4, bf16[2,112,3072]{2,1,0:T(8,128)(2,1)S(1)} %collective-permute-done.4), kind=kLoop, calls=%fused_computation.9 | loop fusion | bytes 1376256 | tf_op jit(solution)/shard_map/dynamic_update_slice | solution.py:230
  69.7 0.9 %fusion.2 = bf16[2,1,128,8192]{3,2,1,0:T(8,128)(2,1)} fusion(bf16[2,1,128,8192]{3,2,1,0:T(8,128)(2,1)} %fusion.3, bf16[2,112,3072]{2,1,0:T(8,128)(2,1)S(1)} %collective-permute-done.4), kind=kLoop, calls=%fused_computation.7 | loop fusion | bytes 1376256 | tf_op jit(solution)/shard_map/dynamic_update_slice | solution.py:230
  70.6 4.9 %collective-permute-done.5 = bf16[2,112,3072]{2,1,0:T(8,128)(2,1)} collective-permute-done((bf16[2,112,3072]{2,1,0:T(8,128)(2,1)}, bf16[2,112,3072]{2,1,0:T(8,128)(2,1)}, u32[]{:S(2)}, u32[]{:S(2)}) %collective-permute-start.5) | collective-permute-done | bytes 1376288 | tf_op jit(solution)/shard_map/ppermute | solution.py:236
  75.6 1.5 %broadcast_select_fusion = bf16[2,112,3072]{2,1,0:T(8,128)(2,1)S(1)} fusion(bf16[2,112,3072]{2,1,0:T(8,128)(2,1)} %collective-permute-done.5, bf16[2,112,3072]{2,1,0:T(8,128)(2,1)S(1)} %collective-permute-done.2, pred[]{:T(512)S(6)} %or.3), kind=kLoop, calls=%fused_computation | loop fusion | flops 688128 | bytes 4128769 | tf_op jit(solution)/shard_map/jit(_where)/select_n | solution.py:271
  77.1 0.9 %fusion.1 = bf16[2,1,128,8192]{3,2,1,0:T(8,128)(2,1)} fusion(bf16[2,1,128,8192]{3,2,1,0:T(8,128)(2,1)} %fusion.2, bf16[2,112,3072]{2,1,0:T(8,128)(2,1)S(1)} %broadcast_select_fusion), kind=kLoop, calls=%fused_computation.5 | loop fusion | bytes 1376256 | tf_op jit(solution)/shard_map/dynamic_update_slice | solution.py:230
  (17 shorter events, 5.1 us)
Async XLA Ops:
  4.6 31.2 %collective-permute-start.3 = (bf16[2,112,2048]{2,1,0:T(8,128)(2,1)}, bf16[2,112,2048]{2,1,0:T(8,128)(2,1)}, u32[]{:S(2)}, u32[]{:S(2)}) collective-permute-start(bf16[2,112,2048]{2,1,0:T(8,128)(2,1)} %get-tuple-element.30), channel_id=1, source_target_pairs={{8,0},{16,8},{24,16},{32,24},{40,32},{48,40},{56,48},{64,56},{72,6... | collective-permute-start | bytes 2752520 | tf_op jit(solution)/shard_map/ppermute | solution.py:236
  11.2 31.5 %collective-permute-start.2 = (bf16[2,112,3072]{2,1,0:T(8,128)(2,1)}, bf16[2,112,3072]{2,1,0:T(8,128)(2,1)S(1)}, u32[]{:S(2)}, u32[]{:S(2)}) collective-permute-start(bf16[2,112,3072]{2,1,0:T(8,128)(2,1)} %get-tuple-element.21), channel_id=1, source_target_pairs={{16,8},{24,16},{32,24},{40,32},{48,40},{56,48},{64,56},{72,64},{80... | collective-permute-start | bytes 4128776 | tf_op jit(solution)/shard_map/ppermute | solution.py:236
  13.5 14.5 %collective-permute-start.1 = (bf16[8,8192]{1,0:T(8,128)(2,1)S(1)}, bf16[8,8192]{1,0:T(8,128)(2,1)S(1)}, u32[]{:S(2)}, u32[]{:S(2)}) collective-permute-start(bf16[8,8192]{1,0:T(8,128)(2,1)S(1)} %multiply_convert_fusion), channel_id=1, source_target_pairs={{1,0},{2,1},{3,2},{4,3},{5,4},{6,5},{7,6},{9,8},{10,9},{11,10},{12... | collective-permute-start | bytes 393224 | tf_op jit(solution)/shard_map/ppermute | solution.py:236
  19.5 8.5 %collective-permute-start = (bf16[8,8192]{1,0:T(8,128)(2,1)S(1)}, bf16[8,8192]{1,0:T(8,128)(2,1)S(1)}, u32[]{:S(2)}, u32[]{:S(2)}) collective-permute-start(bf16[8,8192]{1,0:T(8,128)(2,1)S(1)} %slice.33), channel_id=1, source_target_pairs={{0,1},{1,2},{2,3},{3,4},{4,5},{5,6},{6,7},{8,9},{9,10},{10,11},{11... | collective-permute-start | bytes 393224 | tf_op jit(solution)/shard_map/ppermute | solution.py:236
  26.8 42.1 %collective-permute-start.4 = (bf16[2,112,3072]{2,1,0:T(8,128)(2,1)}, bf16[2,112,3072]{2,1,0:T(8,128)(2,1)S(1)}, u32[]{:S(2)}, u32[]{:S(2)}) collective-permute-start(bf16[2,112,3072]{2,1,0:T(8,128)(2,1)} %get-tuple-element.33), channel_id=1, source_target_pairs={{8,0},{16,8},{24,16},{32,24},{40,32},{48,40},{56,48},{64,56},{72,6... | collective-permute-start | bytes 4128776 | tf_op jit(solution)/shard_map/ppermute | solution.py:236
  28.1 0.7 copy-start
  28.1 0.7 copy-start.1
  34.5 44.4 %collective-permute-start.6 = (bf16[2,16,8192]{2,1,0:T(8,128)(2,1)}, bf16[2,16,8192]{2,1,0:T(8,128)(2,1)S(1)}, u32[]{:S(2)}, u32[]{:S(2)}) collective-permute-start(bf16[2,16,8192]{2,1,0:T(8,128)(2,1)} %get-tuple-element.35), channel_id=1, source_target_pairs={{8,0},{16,8},{24,16},{32,24},{40,32},{48,40},{56,48},{64,56},{72,6... | collective-permute-start | bytes 1572872 | tf_op jit(solution)/shard_map/ppermute | solution.py:236
  44.0 14.6 %all-to-all-start = ((f32[8,7,1024]{2,1,0:T(8,128)}), f32[8,7,1024]{2,1,0:T(8,128)S(1)}, u32[]{:S(2)}, u32[]{:S(2)}) async-start(f32[8,7,1024]{2,1,0:T(8,128)} %get-tuple-element.28), calls=%async_computation | async-start | bytes 524288 | tf_op jit(solution)/shard_map/all_to_all | solution.py:269
  52.1 23.5 %collective-permute-start.5 = (bf16[2,112,3072]{2,1,0:T(8,128)(2,1)}, bf16[2,112,3072]{2,1,0:T(8,128)(2,1)}, u32[]{:S(2)}, u32[]{:S(2)}) collective-permute-start(bf16[2,112,3072]{2,1,0:T(8,128)(2,1)} %broadcast_select_fusion.1), channel_id=1, source_target_pairs={{0,120},{8,0},{1,121},{9,1},{2,122},{10,2},{3,123},{11,3},{4,124},... | collective-permute-start | bytes 4128776 | tf_op jit(solution)/shard_map/ppermute | solution.py:236
  60.0 20.4 %collective-permute-start.7 = (f32[1,7,1024]{2,0,1:T(1,128)S(1)}, f32[1,7,1024]{2,0,1:T(1,128)S(1)}, u32[]{:S(2)}, u32[]{:S(2)}) collective-permute-start(f32[1,7,1024]{2,0,1:T(1,128)S(1)} %broadcast_in_dim.3), channel_id=1, source_target_pairs={{0,248},{8,240},{16,232},{24,224},{32,216},{40,208},{48,200},{56,1... | collective-permute-start | bytes 86024 | tf_op jit(solution)/shard_map/ppermute | solution.py:236
where the time goes:
time: 81.8 us; the launch traced here: 80.9 us
  starting transfers between devices  33.8 us (41%)
  Pallas kernels  20.3 us (25%)
  local copies, waits for them, and re-layouts  11 us (13%)
  waiting for transfers between devices  10 us (12%)
  other arithmetic  4.99 us (6%)
    ppermute x8, starting transfers between devices, sent(): lax.ppermute(x, axis, [(i, to(i)) for i in range(n) if 0 <= to(i) < n])  27.5 us
    pallas_call x3, Pallas kernels, main_part(): pl.pallas_call(functools.partial(main_kernel, taps), out_shape=(jax.Shape...  14.6 us
    ppermute x8, waiting for transfers between devices, sent(): lax.ppermute(x, axis, [(i, to(i)) for i in range(n) if 0 <= to(i) < n])  10 us
    dynamic_update_slice x8, local copies, waits for them, and re-layouts, put(): out = lax.dynamic_update_slice(out, y[k][None, None], (k, 0, row, lane))  8.66 us
    all_to_all x1, starting transfers between devices, local(): shares = lax.all_to_all(dh, 'ctx', split_axis=0, concat_axis=0, tiled=True)  6.31 us
    pallas_call x1, Pallas kernels, edge_part(): pl.pallas_call(functools.partial(edge_kernel, taps, rows), out_shape=(jax...  5.72 us
  transfers between devices with their start and end apart: 9, of which 2 were waited for; matrix products, arithmetic and copies ran while one was open for 18% of the time, Pallas kernels for 20%

commit v1 on v0

--- a/solution.py
+++ b/solution.py
@@ -12,7 +12,7 @@
 LANES = 128
 EDGE = 16
 HALO = 8
-RANGES = ((2, 1024), (3, 1024), (3, 1024))
+RANGES = ((3, 1024), (3, 1024), (2, 1024))
 
 
 def f32(x):
@@ -62,16 +62,16 @@
     return lengths_ref[0, 0] - ctx * rows
 
 
-def by_boundary(cut, rows, taps, body, count):
+def by_boundary(cut, rows, taps, body, count, unroll=1):
     near = (cut > -taps) & (cut < rows + taps)
 
     @pl.when(near)
     def _():
-        lax.fori_loop(0, count, functools.partial(body, True), 0)
+        lax.fori_loop(0, count, functools.partial(body, True), 0, unroll=unroll)
 
     @pl.when(jnp.logical_not(near))
     def _():
-        lax.fori_loop(0, count, functools.partial(body, False), 0)
+        lax.fori_loop(0, count, functools.partial(body, False), 0, unroll=unroll)
 
 
 def main_kernel(taps, lengths_ref, f_ref, q_ref, u_ref, g_ref, *rest):
@@ -160,7 +160,7 @@
             dh_sums[dest, pl.ds(j, 1), place] = dh_sums[dest, pl.ds(j, 1), place] + jnp.sum(acc[j], axis=0, keepdims=True)
         return carry
 
-    by_boundary(cut, rows, taps, column, q_lo.shape[1] // LANES)
+    by_boundary(cut, rows, taps, column, q_lo.shape[1] // LANES, unroll=4)
     copies = [pltpu.make_async_copy(y_ref, y_hbm, sems.at[0]), pltpu.make_async_copy(dh_sums, dh_out, sems.at[1])]
     for copy in copies:
         copy.start()
@@ -243,38 +243,39 @@
     shards = lax.axis_size("ctx")
     eighth = width // sum(part for part, _ in RANGES)
 
-    first, dh, parts = 0, None, []
-    for part, block in RANGES:
-        count = part * eighth
-        y, dh, blank = main_part(trace_lengths, f3, query, inner, out_grad, dh, shards, first, count, block)
-        out = blank if first == 0 else out
+    pipe, half = lax.axis_index("pipe"), lax.axis_size("pipe") // 2
+    back = lambda i: i - 1
+    dh, parts, first = None, [], 0
+    for n, (part, block) in enumerate(RANGES):
+        if n == 2:
+            dh, out, _, _ = lax.optimization_barrier((dh, out, u_tail, gz_head))
+        y, dh, blank = main_part(trace_lengths, f3, query, inner, out_grad, dh, shards, first, part * eighth, block)
+        if n == 0:
+            out = blank
         parts.append((first, y))
-        first += count
-    pipe, half = lax.axis_index("pipe"), lax.axis_size("pipe") // 2
-    arrived = [(first, sent(y, "pipe", lambda i: i - 1)) for first, y in parts]
-    y_two = parts[1][1]
-    near = sent(y_two, "pipe", lambda i: 0 if i == half else i - 1 if i > 1 else -1)
-    relay = jnp.where(pipe == 0, near, y_two)
-
-    q_head, g_head, u_tail, _ = lax.optimization_barrier((query, out_grad, inner, parts[1][1]))
-    left = sent(u_tail[rows - HALO :], "ctx", lambda i: i + 1)
-    right = sent((f32(g_head[:HALO]) * f32(q_head[:HALO])).astype(jnp.bfloat16), "ctx", lambda i: i - 1)
-    f0, y0 = arrived[0]
-    out = put(out, y0, ((EDGE, f0), (0, f0)))
+        first += part * eighth
+        if n == 1:
+            (f0, y0), (f1, y_two) = parts
+            a0 = sent(y0, "pipe", back)
+            near = sent(y_two, "pipe", lambda i: 0 if i == half else i - 1 if i > 1 else -1)
+            relay = jnp.where(pipe == 0, near, y_two)
+            q_head, g_head, u_tail, _ = lax.optimization_barrier((query, out_grad, inner, y_two))
+            u_tail = u_tail[rows - HALO :]
+            gz_head = (f32(g_head[:HALO]) * f32(q_head[:HALO])).astype(jnp.bfloat16)
+            left, right = sent(u_tail, "ctx", lambda i: i + 1), sent(gz_head, "ctx", back)
+            out = put(out, a0, ((EDGE, f0), (0, f0)))
+    f2, a2 = parts[2][0], sent(parts[2][1], "pipe", back)
     y_edge, dh = edge_part(trace_lengths, f3, query, inner, out_grad, left, right, dh)
-    edge = sent(y_edge, "pipe", lambda i: i - 1)
-
+    edge = sent(y_edge, "pipe", back)
     dh, relay = lax.optimization_barrier((dh, relay))
     far = sent(relay, "pipe", lambda i: half - 1 if i == 0 else 0 if i == 1 else -1)
     shares = lax.all_to_all(dh, "ctx", split_axis=0, concat_axis=0, tiled=True)
+    out = put(out, a2, ((EDGE, f2), (0, f2)))
     shares, out = lax.optimization_barrier((shares, out))
-    arrived = [arrived[2], (arrived[1][0], jnp.where((pipe == 0) | (pipe == half - 1), far, near))]
     mine = jnp.sum(shares, axis=0)[None]
     last = lax.axis_size("pipe") - 1
     theirs = sent(mine, "pipe", lambda i: last - i)
-
-    for first, y in arrived:
-        out = put(out, y, ((EDGE, first), (0, first)))
+    out = put(out, jnp.where((pipe == 0) | (pipe == half - 1), far, near), ((EDGE, f1), (0, f1)))
     out = put(out, edge, ((0, 0), (rows - EDGE, 0)))
     mine, out = lax.optimization_barrier((mine, out))
     return out, mine + theirs

time: 81.8 us -> 76.4 us (0.934)
  starting transfers between devices: 33.8 us -> 27.2 us
  waiting for transfers between devices: 10 us -> 12.6 us
  other arithmetic: 4.99 us -> 3.67 us
    ppermute x8, starting transfers between devices: 27.5 us -> 22.1 us  [sent(): lax.ppermute(x, axis, [(i, to(i)) for i in range(n) if 0 <= to(i) < n])]
    ppermute x8, waiting for transfers between devices: 10 us -> 12.4 us  [sent(): lax.ppermute(x, axis, [(i, to(i)) for i in range(n) if 0 <= to(i) < n])]
    select_n x1, other arithmetic: 1.48 us -> 0.14 us  [local(): jnp.where((pipe == 0) | (pipe == half - 1), far, near)]
    all_to_all x1, starting transfers between devices: 6.31 us -> 5.07 us  [local(): shares = lax.all_to_all(dh, 'ctx', split_axis=0, concat_axis=0, tiled=True)]
  transfers between devices with their start and end apart: 9 -> 9, of which waited for: 2 -> 3; matrix products, arithmetic and copies ran while one was open for 18% -> 18% of each run, Pallas kernels for 20% -> 19%
where the time goes in v1:
time: 76.4 us; the launch traced here: 75 us
  starting transfers between devices  27.2 us (36%)
  Pallas kernels  19.7 us (26%)
  waiting for transfers between devices  12.6 us (16%)
  local copies, waits for them, and re-layouts  11.1 us (15%)
  other arithmetic  3.67 us (5%)
  between operations  0.78 us (1%)
    ppermute x8, starting transfers between devices, sent(): lax.ppermute(x, axis, [(i, to(i)) for i in range(n) if 0 <= to(i) < n])  22.1 us
    pallas_call x3, Pallas kernels, main_part(): pl.pallas_call(functools.partial(main_kernel, taps), out_shape=(jax.Shape...  14.6 us
    ppermute x8, waiting for transfers between devices, sent(): lax.ppermute(x, axis, [(i, to(i)) for i in range(n) if 0 <= to(i) < n])  12.4 us
    dynamic_update_slice x8, local copies, waits for them, and re-layouts, put(): out = lax.dynamic_update_slice(out, y[k][None, None], (k, 0, row, lane))  8.67 us
    pallas_call x1, Pallas kernels, edge_part(): pl.pallas_call(functools.partial(edge_kernel, taps, rows), out_shape=(jax...  5.13 us
    all_to_all x1, starting transfers between devices, local(): shares = lax.all_to_all(dh, 'ctx', split_axis=0, concat_axis=0, tiled=True)  5.07 us
  transfers between devices with their start and end apart: 9, of which 3 were waited for; matrix products, arithmetic and copies ran while one was open for 18% of the time, Pallas kernels for 19%

profile of v1, /device:TPU:2, one launch (start us, length us, event | category | flops | bytes accessed | tf_op | source)
XLA Modules:
  0.0 75.0 jit_solution(4963813054833466911)
XLA Ops:
  0.6 5.3 %grads_0.1 = (bf16[2,112,3072]{2,1,0:T(8,128)(2,1)}, f32[8,7,1024]{2,1,0:T(8,128)}, bf16[2,1,128,8192]{3,2,1,0:T(8,128)(2,1)}) custom-call(s32[1,2]{1,0:T(1,128)} %lengths_ref.7, f32[7,1,8192]{2,1,0:T(1,128)} %bitcast.51, bf16[128,8192]{1,0:T(8,128)(2,1)} %bitcast.36, bf16[128,8192]{1,0:T(8,128)(2,1)} %bitcast.41, bf16[128,8192]{1,0:T(8,128)(2,1)} %bitcast.46), custom_call_target="tpu_custom_call" | custom-call | flops 1 | bytes 1 | tf_op jit(solution)/shard_map/grads_0/pallas_call | solution.py:184
  5.9 1.3 %collective-permute-start.2 = (bf16[2,112,3072]{2,1,0:T(8,128)(2,1)}, bf16[2,112,3072]{2,1,0:T(8,128)(2,1)S(1)}, u32[]{:S(2)}, u32[]{:S(2)}) collective-permute-start(bf16[2,112,3072]{2,1,0:T(8,128)(2,1)} %get-tuple-element.29), channel_id=1, source_target_pairs={{8,0},{16,8},{24,16},{32,24},{40,32},{48,40},{56,48},{64,56},{72,6... | collective-permute-start | bytes 4128776 | tf_op jit(solution)/shard_map/ppermute | solution.py:236
  7.2 5.3 %grads_3072.1 = (bf16[2,112,3072]{2,1,0:T(8,128)(2,1)}, f32[8,7,1024]{2,1,0:T(8,128)}, bf16[1,1,8,128]{3,2,1,0:T(8,128)(2,1)}) custom-call(s32[1,2]{1,0:T(1,128)} %lengths_ref.7, f32[7,1,8192]{2,1,0:T(1,128)} %bitcast.52, bf16[128,8192]{1,0:T(8,128)(2,1)} %bitcast.37, bf16[128,8192]{1,0:T(8,128)(2,1)} %bitcast.42, ...), custom_call_target="tpu_custom_call", output_to_operand_aliasing={{1}: (5, {})} | custom-call | flops 1 | bytes 1 | tf_op jit(solution)/shard_map/grads_3072/pallas_call | solution.py:184
  12.5 1.3 %collective-permute-start.3 = (bf16[2,112,3072]{2,1,0:T(8,128)(2,1)}, bf16[2,112,3072]{2,1,0:T(8,128)(2,1)S(1)}, u32[]{:S(2)}, u32[]{:S(2)}) collective-permute-start(bf16[2,112,3072]{2,1,0:T(8,128)(2,1)} %get-tuple-element.23), channel_id=1, source_target_pairs={{16,8},{24,16},{32,24},{40,32},{48,40},{56,48},{64,56},{72,64},{80... | collective-permute-start | bytes 4128776 | tf_op jit(solution)/shard_map/ppermute | solution.py:236
  13.8 1.0 %multiply_convert_fusion = bf16[8,8192]{1,0:T(8,128)(2,1)S(1)} fusion(bf16[128,8192]{1,0:T(8,128)(2,1)} %bitcast.38, bf16[128,8192]{1,0:T(8,128)(2,1)} %bitcast.48), kind=kLoop, calls=%fused_computation.18 | loop fusion | flops 262144 | bytes 393216 | tf_op jit(solution)/shard_map/convert_element_type | solution.py:264
  14.8 3.5 %collective-permute-start.1 = (bf16[8,8192]{1,0:T(8,128)(2,1)S(1)}, bf16[8,8192]{1,0:T(8,128)(2,1)S(1)}, u32[]{:S(2)}, u32[]{:S(2)}) collective-permute-start(bf16[8,8192]{1,0:T(8,128)(2,1)S(1)} %multiply_convert_fusion), channel_id=1, source_target_pairs={{1,0},{2,1},{3,2},{4,3},{5,4},{6,5},{7,6},{9,8},{10,9},{11,10},{12... | collective-permute-start | bytes 393224 | tf_op jit(solution)/shard_map/ppermute | solution.py:236
  18.3 0.9 %slice.33 = bf16[8,8192]{1,0:T(8,128)(2,1)S(1)} slice(bf16[128,8192]{1,0:T(8,128)(2,1)} %bitcast.43), slice={[120:128], [0:8192]} | slice | bytes 262144 | tf_op jit(solution)/shard_map/slice | solution.py:263
  19.2 3.7 %collective-permute-start = (bf16[8,8192]{1,0:T(8,128)(2,1)S(1)}, bf16[8,8192]{1,0:T(8,128)(2,1)S(1)}, u32[]{:S(2)}, u32[]{:S(2)}) collective-permute-start(bf16[8,8192]{1,0:T(8,128)(2,1)S(1)} %slice.33), channel_id=1, source_target_pairs={{0,1},{1,2},{2,3},{3,4},{4,5},{5,6},{6,7},{8,9},{9,10},{10,11},{11... | collective-permute-start | bytes 393224 | tf_op jit(solution)/shard_map/ppermute | solution.py:236
  22.9 0.9 %fusion.3 = bf16[2,1,128,8192]{3,2,1,0:T(8,128)(2,1)} fusion(bf16[2,1,128,8192]{3,2,1,0:T(8,128)(2,1)} %get-tuple-element.28, bf16[2,112,3072]{2,1,0:T(8,128)(2,1)S(1)} %collective-permute-done.2), kind=kLoop, calls=%fused_computation.9 | loop fusion | bytes 1376256 | tf_op jit(solution)/shard_map/dynamic_update_slice | solution.py:230
  23.8 0.9 %fusion.2 = bf16[2,1,128,8192]{3,2,1,0:T(8,128)(2,1)} fusion(bf16[2,1,128,8192]{3,2,1,0:T(8,128)(2,1)} %fusion.3, bf16[2,112,3072]{2,1,0:T(8,128)(2,1)S(1)} %collective-permute-done.2), kind=kLoop, calls=%fused_computation.7 | loop fusion | bytes 1376256 | tf_op jit(solution)/shard_map/dynamic_update_slice | solution.py:230
  24.7 4.0 %grads_6144.1 = (bf16[2,112,2048]{2,1,0:T(8,128)(2,1)}, f32[8,7,1024]{2,1,0:T(8,128)}, bf16[1,1,8,128]{3,2,1,0:T(8,128)(2,1)}) custom-call(s32[1,2]{1,0:T(1,128)} %lengths_ref.7, f32[7,1,8192]{2,1,0:T(1,128)} %bitcast.53, bf16[128,8192]{1,0:T(8,128)(2,1)} %bitcast.39, bf16[128,8192]{1,0:T(8,128)(2,1)} %bitcast.44, ...), custom_call_target="tpu_custom_call", output_to_operand_aliasing={{1}: (5, {})} | custom-call | flops 1 | bytes 1 | tf_op jit(solution)/shard_map/grads_6144/pallas_call | solution.py:184
  28.7 1.4 %collective-permute-start.4 = (bf16[2,112,2048]{2,1,0:T(8,128)(2,1)}, bf16[2,112,2048]{2,1,0:T(8,128)(2,1)}, u32[]{:S(2)}, u32[]{:S(2)}) collective-permute-start(bf16[2,112,2048]{2,1,0:T(8,128)(2,1)} %get-tuple-element.35), channel_id=1, source_target_pairs={{8,0},{16,8},{24,16},{32,24},{40,32},{48,40},{56,48},{64,56},{72,6... | collective-permute-start | bytes 2752520 | tf_op jit(solution)/shard_map/ppermute | solution.py:236
  30.9 5.1 %edge_grads.1 = (bf16[2,16,8192]{2,1,0:T(8,128)(2,1)}, f32[8,7,1024]{2,1,0:T(8,128)}) custom-call(s32[1,2]{1,0:T(1,128)} %lengths_ref.7, f32[7,1,8192]{2,1,0:T(1,128)} %bitcast.54, bf16[128,8192]{1,0:T(8,128)(2,1)} %bitcast.40, bf16[128,8192]{1,0:T(8,128)(2,1)} %bitcast.45, bf16[128,8192]{1,0:T(8,128)(2,1)} %bitcast.50, bf16[8,8192]{1,0:T(8,128)(2,1)} %copy-done.2, ...), custom_call_target="tpu_custom_call" | custom-call | flops 1 | bytes 1 | tf_op jit(solution)/shard_map/edge_grads/pallas_call | solution.py:210
  36.0 8.0 %collective-permute-done.3 = bf16[2,112,3072]{2,1,0:T(8,128)(2,1)S(1)} collective-permute-done((bf16[2,112,3072]{2,1,0:T(8,128)(2,1)}, bf16[2,112,3072]{2,1,0:T(8,128)(2,1)S(1)}, u32[]{:S(2)}, u32[]{:S(2)}) %collective-permute-start.3) | collective-permute-done | bytes 1376288 | tf_op jit(solution)/shard_map/ppermute | solution.py:236
  44.0 1.3 %broadcast_select_fusion.1 = bf16[2,112,3072]{2,1,0:T(8,128)(2,1)} fusion(bf16[2,112,3072]{2,1,0:T(8,128)(2,1)S(1)} %collective-permute-done.3, bf16[2,112,3072]{2,1,0:T(8,128)(2,1)S(1)} %copy-done, pred[]{:T(512)S(6)} %eq.7), kind=kLoop, calls=%fused_computation.1 | loop fusion | flops 688128 | bytes 4128769 | tf_op jit(solution)/shard_map/jit(_where)/select_n | solution.py:261
  45.3 8.7 %collective-permute-start.5 = (bf16[2,112,3072]{2,1,0:T(8,128)(2,1)}, bf16[2,112,3072]{2,1,0:T(8,128)(2,1)S(1)}, u32[]{:S(2)}, u32[]{:S(2)}) collective-permute-start(bf16[2,112,3072]{2,1,0:T(8,128)(2,1)} %broadcast_select_fusion.1), channel_id=1, source_target_pairs={{0,120},{8,0},{1,121},{9,1},{2,122},{10,2},{3,123},{11,3},{4,124},... | collective-permute-start | bytes 4128776 | tf_op jit(solution)/shard_map/ppermute | solution.py:236
  54.0 5.1 %all-to-all-start = ((f32[8,7,1024]{2,1,0:T(8,128)}), f32[8,7,1024]{2,1,0:T(8,128)S(1)}, u32[]{:S(2)}, u32[]{:S(2)}) async-start(f32[8,7,1024]{2,1,0:T(8,128)} %get-tuple-element.33), calls=%async_computation | async-start | bytes 524288 | tf_op jit(solution)/shard_map/all_to_all | solution.py:272
  59.0 1.3 %collective-permute-start.6 = (bf16[2,16,8192]{2,1,0:T(8,128)(2,1)}, bf16[2,16,8192]{2,1,0:T(8,128)(2,1)S(1)}, u32[]{:S(2)}, u32[]{:S(2)}) collective-permute-start(bf16[2,16,8192]{2,1,0:T(8,128)(2,1)} %get-tuple-element.39), channel_id=1, source_target_pairs={{8,0},{16,8},{24,16},{32,24},{40,32},{48,40},{56,48},{64,56},{72,6... | collective-permute-start | bytes 1572872 | tf_op jit(solution)/shard_map/ppermute | solution.py:236
  60.3 1.8 %fusion.5 = bf16[2,1,128,8192]{3,2,1,0:T(8,128)(2,1)} fusion(bf16[2,1,128,8192]{3,2,1,0:T(8,128)(2,1)} %fusion.2, bf16[2,112,2048]{2,1,0:T(8,128)(2,1)} %collective-permute-done.4), kind=kLoop, calls=%fused_computation.13 | loop fusion | bytes 917504 | tf_op jit(solution)/shard_map/dynamic_update_slice | solution.py:230
  62.2 1.8 %fusion.4 = bf16[2,1,128,8192]{3,2,1,0:T(8,128)(2,1)} fusion(bf16[2,1,128,8192]{3,2,1,0:T(8,128)(2,1)} %fusion.5, bf16[2,112,2048]{2,1,0:T(8,128)(2,1)} %collective-permute-done.4), kind=kLoop, calls=%fused_computation.11 | loop fusion | bytes 917504 | tf_op jit(solution)/shard_map/dynamic_update_slice | solution.py:230
  65.7 1.0 %collective-permute-start.7 = (f32[1,7,1024]{2,0,1:T(1,128)S(1)}, f32[1,7,1024]{2,0,1:T(1,128)S(1)}, u32[]{:S(2)}, u32[]{:S(2)}) collective-permute-start(f32[1,7,1024]{2,0,1:T(1,128)S(1)} %broadcast_in_dim.3), channel_id=1, source_target_pairs={{0,248},{8,240},{16,232},{24,224},{32,216},{40,208},{48,200},{56,1... | collective-permute-start | bytes 86024 | tf_op jit(solution)/shard_map/ppermute | solution.py:236
  66.7 4.3 %collective-permute-done.5 = bf16[2,112,3072]{2,1,0:T(8,128)(2,1)S(1)} collective-permute-done((bf16[2,112,3072]{2,1,0:T(8,128)(2,1)}, bf16[2,112,3072]{2,1,0:T(8,128)(2,1)S(1)}, u32[]{:S(2)}, u32[]{:S(2)}) %collective-permute-start.5) | collective-permute-done | bytes 1376288 | tf_op jit(solution)/shard_map/ppermute | solution.py:236
  71.1 0.9 %fusion.1 = bf16[2,1,128,8192]{3,2,1,0:T(8,128)(2,1)} fusion(bf16[2,1,128,8192]{3,2,1,0:T(8,128)(2,1)} %fusion.4, bf16[2,112,3072]{2,1,0:T(8,128)(2,1)S(1)} %broadcast_select_fusion), kind=kLoop, calls=%fused_computation.5 | loop fusion | bytes 1376256 | tf_op jit(solution)/shard_map/dynamic_update_slice | solution.py:230
  72.0 0.9 %fusion = bf16[2,1,128,8192]{3,2,1,0:T(8,128)(2,1)} fusion(bf16[2,1,128,8192]{3,2,1,0:T(8,128)(2,1)} %fusion.1, bf16[2,112,3072]{2,1,0:T(8,128)(2,1)S(1)} %broadcast_select_fusion), kind=kLoop, calls=%fused_computation.3 | loop fusion | bytes 1376256 | tf_op jit(solution)/shard_map/dynamic_update_slice | solution.py:230
  (19 shorter events, 4.6 us)
Async XLA Ops:
  5.9 17.0 %collective-permute-start.2 = (bf16[2,112,3072]{2,1,0:T(8,128)(2,1)}, bf16[2,112,3072]{2,1,0:T(8,128)(2,1)S(1)}, u32[]{:S(2)}, u32[]{:S(2)}) collective-permute-start(bf16[2,112,3072]{2,1,0:T(8,128)(2,1)} %get-tuple-element.29), channel_id=1, source_target_pairs={{8,0},{16,8},{24,16},{32,24},{40,32},{48,40},{56,48},{64,56},{72,6... | collective-permute-start | bytes 4128776 | tf_op jit(solution)/shard_map/ppermute | solution.py:236
  12.5 31.5 %collective-permute-start.3 = (bf16[2,112,3072]{2,1,0:T(8,128)(2,1)}, bf16[2,112,3072]{2,1,0:T(8,128)(2,1)S(1)}, u32[]{:S(2)}, u32[]{:S(2)}) collective-permute-start(bf16[2,112,3072]{2,1,0:T(8,128)(2,1)} %get-tuple-element.23), channel_id=1, source_target_pairs={{16,8},{24,16},{32,24},{40,32},{48,40},{56,48},{64,56},{72,64},{80... | collective-permute-start | bytes 4128776 | tf_op jit(solution)/shard_map/ppermute | solution.py:236
  14.8 15.3 %collective-permute-start.1 = (bf16[8,8192]{1,0:T(8,128)(2,1)S(1)}, bf16[8,8192]{1,0:T(8,128)(2,1)S(1)}, u32[]{:S(2)}, u32[]{:S(2)}) collective-permute-start(bf16[8,8192]{1,0:T(8,128)(2,1)S(1)} %multiply_convert_fusion), channel_id=1, source_target_pairs={{1,0},{2,1},{3,2},{4,3},{5,4},{6,5},{7,6},{9,8},{10,9},{11,10},{12... | collective-permute-start | bytes 393224 | tf_op jit(solution)/shard_map/ppermute | solution.py:236
  19.2 10.9 %collective-permute-start = (bf16[8,8192]{1,0:T(8,128)(2,1)S(1)}, bf16[8,8192]{1,0:T(8,128)(2,1)S(1)}, u32[]{:S(2)}, u32[]{:S(2)}) collective-permute-start(bf16[8,8192]{1,0:T(8,128)(2,1)S(1)} %slice.33), channel_id=1, source_target_pairs={{0,1},{1,2},{2,3},{3,4},{4,5},{5,6},{6,7},{8,9},{9,10},{10,11},{11... | collective-permute-start | bytes 393224 | tf_op jit(solution)/shard_map/ppermute | solution.py:236
  28.7 15.3 %copy-start = (bf16[2,112,3072]{2,1,0:T(8,128)(2,1)S(1)}, bf16[2,112,3072]{2,1,0:T(8,128)(2,1)}, u32[]{:S(2)}) copy-start(bf16[2,112,3072]{2,1,0:T(8,128)(2,1)} %get-tuple-element.23) | copy-start | bytes 4128772
  28.7 31.6 %collective-permute-start.4 = (bf16[2,112,2048]{2,1,0:T(8,128)(2,1)}, bf16[2,112,2048]{2,1,0:T(8,128)(2,1)}, u32[]{:S(2)}, u32[]{:S(2)}) collective-permute-start(bf16[2,112,2048]{2,1,0:T(8,128)(2,1)} %get-tuple-element.35), channel_id=1, source_target_pairs={{8,0},{16,8},{24,16},{32,24},{40,32},{48,40},{56,48},{64,56},{72,6... | collective-permute-start | bytes 2752520 | tf_op jit(solution)/shard_map/ppermute | solution.py:236
  30.1 0.7 copy-start.1
  30.2 0.7 copy-start.2
  45.3 25.7 %collective-permute-start.5 = (bf16[2,112,3072]{2,1,0:T(8,128)(2,1)}, bf16[2,112,3072]{2,1,0:T(8,128)(2,1)S(1)}, u32[]{:S(2)}, u32[]{:S(2)}) collective-permute-start(bf16[2,112,3072]{2,1,0:T(8,128)(2,1)} %broadcast_select_fusion.1), channel_id=1, source_target_pairs={{0,120},{8,0},{1,121},{9,1},{2,122},{10,2},{3,123},{11,3},{4,124},... | collective-permute-start | bytes 4128776 | tf_op jit(solution)/shard_map/ppermute | solution.py:236
  54.0 10.3 %all-to-all-start = ((f32[8,7,1024]{2,1,0:T(8,128)}), f32[8,7,1024]{2,1,0:T(8,128)S(1)}, u32[]{:S(2)}, u32[]{:S(2)}) async-start(f32[8,7,1024]{2,1,0:T(8,128)} %get-tuple-element.33), calls=%async_computation | async-start | bytes 524288 | tf_op jit(solution)/shard_map/all_to_all | solution.py:272
  59.0 13.9 %collective-permute-start.6 = (bf16[2,16,8192]{2,1,0:T(8,128)(2,1)}, bf16[2,16,8192]{2,1,0:T(8,128)(2,1)S(1)}, u32[]{:S(2)}, u32[]{:S(2)}) collective-permute-start(bf16[2,16,8192]{2,1,0:T(8,128)(2,1)} %get-tuple-element.39), channel_id=1, source_target_pairs={{8,0},{16,8},{24,16},{32,24},{40,32},{48,40},{56,48},{64,56},{72,6... | collective-permute-start | bytes 1572872 | tf_op jit(solution)/shard_map/ppermute | solution.py:236
  65.7 8.7 %collective-permute-start.7 = (f32[1,7,1024]{2,0,1:T(1,128)S(1)}, f32[1,7,1024]{2,0,1:T(1,128)S(1)}, u32[]{:S(2)}, u32[]{:S(2)}) collective-permute-start(f32[1,7,1024]{2,0,1:T(1,128)S(1)} %broadcast_in_dim.3), channel_id=1, source_target_pairs={{0,248},{8,240},{16,232},{24,224},{32,216},{40,208},{48,200},{56,1... | collective-permute-start | bytes 86024 | tf_op jit(solution)/shard_map/ppermute | solution.py:236
